TPU v7x, 128 devices: a whole 4x4x4 slice. The times are simulated.
128 devices in a mesh: tile: 16 (over y, x_lo, core), head: 8 (over x_hi, z).
Axes of the slice: x: 4 (x_hi: 2, x_lo: 2; x = x_hi * 2 + x_lo), y: 4, z: 4, core: 2. Of those that a mesh axis runs over, the one named last changes fastest.
Arguments:
- cells: bfloat16 [16, 12, 640, 1024], P('tile', None, None, 'head'), may hold values from -8 to 8
- conv_weight: float32 [9, 1024], P(None, 'head'), may hold values from -2 to 2
- qkv_weight: bfloat16 [3, 1024, 1024], P(None, None, 'head'), may hold values from -0.1875 to 0.1875
- out_weight: bfloat16 [1024, 1024], P(None, 'head'), may hold values from -0.1875 to 0.1875
- block_mask: int32 [6, 20], replicated, may hold values 0 or 1
Outputs:
- result: bfloat16 [16, 12, 640, 1024], P('tile', None, None, 'head')
All inputs are finite; a program needn't handle non-finite values.
Results may differ from a plain program's by a relative error of at most 0.012.
The roundings to bfloat16 on the way count: a program that leaves them out, or rounds other values in their place, can miss the bound.
Values may be sent and summed in bfloat16 or wider, within the bound.
A program may use at most 128 MiB of HBM per device.

v0:
```python
import jax
import jax.numpy as jnp
from jax import lax
from jax.sharding import PartitionSpec as P

HEAD_DIM = 64
WIN = 7
TILE = 32
RADIUS = 3


def passed_along(block, axis, distance):
    devices = range(lax.axis_size(axis))
    route = [(i - distance, i) for i in devices if i - distance in devices]
    return lax.ppermute(block, axis, route)


def tile_occupancy(block_mask):
    tile_rows = block_mask.shape[0]
    tile_cols = block_mask.shape[1]
    spread = jnp.broadcast_to(block_mask[:, None, :, None], (tile_rows, TILE, tile_cols, TILE))
    return spread.reshape(tile_rows * TILE, tile_cols * TILE)


def rim_both(block, width):
    row_dim = block.ndim - 3
    col_dim = block.ndim - 2
    row_total = block.shape[row_dim]
    top_rows = lax.slice_in_dim(block, 0, width, axis=row_dim)
    bottom_rows = lax.slice_in_dim(block, row_total - width, row_total, axis=row_dim)
    from_above = passed_along(bottom_rows, "tile", 1)
    from_below = passed_along(top_rows, "tile", -1)
    taller = jnp.concatenate([from_above, block, from_below], axis=row_dim)
    pad_spec = [(0, 0)] * block.ndim
    pad_spec[col_dim] = (width, width)
    return jnp.pad(taller, pad_spec)


def conv_mix(extended, conv_weight):
    values = extended.astype(jnp.float32)
    out_rows = extended.shape[0] - 2
    out_cols = extended.shape[1] - 2
    running = values[1:-1, 1:-1]
    for row_off in range(3):
        for col_off in range(3):
            running = (
                running
                + conv_weight[3 * row_off + col_off]
                * values[row_off : row_off + out_rows, col_off : col_off + out_cols]
            )
    return running.astype(jnp.bfloat16)


def attend(queries, keyvals, near_occ):
    row_count, col_count, chan_count = queries.shape
    local_heads = chan_count // HEAD_DIM
    query_parts = queries.reshape(row_count, col_count, local_heads, HEAD_DIM)
    padded = keyvals.reshape(
        2, row_count + 2 * RADIUS, col_count + 2 * RADIUS, local_heads, HEAD_DIM
    )
    score_scale = HEAD_DIM ** (-0.5)
    score_list = []
    allowed_list = []
    for row_off in range(WIN):
        for col_off in range(WIN):
            key_part = padded[0, row_off : row_off + row_count, col_off : col_off + col_count]
            score_list.append(
                jnp.einsum(
                    "rchd,rchd->hrc", query_parts, key_part, preferred_element_type=jnp.float32
                )
                * score_scale
            )
            if row_off == RADIUS and col_off == RADIUS:
                allowed_list.append(jnp.ones((row_count, col_count), dtype=bool))
            else:
                allowed_list.append(
                    near_occ[row_off : row_off + row_count, col_off : col_off + col_count] > 0
                )
    scores = jnp.stack(score_list)
    allowed = jnp.stack(allowed_list)[:, None]
    masked = jnp.where(allowed, scores, jnp.float32(-1e30))
    row_peak = jnp.max(masked, axis=0)
    exp_scores = jnp.exp(masked - row_peak)
    weights = (exp_scores / jnp.sum(exp_scores, axis=0)).astype(jnp.bfloat16)
    running = jnp.zeros((row_count, col_count, local_heads, HEAD_DIM), jnp.float32)
    for row_off in range(WIN):
        for col_off in range(WIN):
            position = row_off * WIN + col_off
            value_part = padded[1, row_off : row_off + row_count, col_off : col_off + col_count]
            running = running + jnp.einsum(
                "hrc,rchd->rchd", weights[position], value_part, preferred_element_type=jnp.float32
            )
    return running.reshape(row_count, col_count, chan_count).astype(jnp.bfloat16)


def per_device(cells, conv_weight, qkv_weight, out_weight, block_mask):
    own_cells = cells[0]
    row_count, col_count, chan_count = own_cells.shape
    place = lax.axis_index("tile")
    start_row = place * row_count
    occupancy = jnp.pad(tile_occupancy(block_mask), RADIUS)
    near_occ = lax.dynamic_slice(
        occupancy, (start_row, 0), (row_count + 2 * RADIUS, col_count + 2 * RADIUS)
    )
    extended = rim_both(own_cells, 1)
    mixed = conv_mix(extended, conv_weight)
    weights = qkv_weight
    projected = jnp.einsum(
        "rck,tkh->trch",
        lax.all_gather(mixed, "head", axis=2, tiled=True),
        weights,
        preferred_element_type=jnp.float32,
    ).astype(jnp.bfloat16)
    queries = projected[0]
    keyvals = rim_both(projected[1:], RADIUS)
    attended = attend(queries, keyvals, near_occ)
    weights = out_weight
    final_proj = jnp.einsum(
        "rck,kh->rch",
        lax.all_gather(attended, "head", axis=2, tiled=True),
        weights,
        preferred_element_type=jnp.float32,
    )
    return (own_cells.astype(jnp.float32) + final_proj).astype(jnp.bfloat16)[None]


def solution(mesh):
    placed = (
        P("tile", None, None, "head"),
        P(None, "head"),
        P(None, None, "head"),
        P(None, "head"),
        P(),
    )
    return jax.shard_map(
        per_device,
        mesh=mesh,
        in_specs=placed,
        out_specs=P("tile", None, None, "head"),
        check_vma=False,
    )
```

profile of v0, /device:TPU:3, one launch (start us, length us, event | category | flops | bytes accessed | tf_op | source)
XLA Modules:
  0.0 557.1 jit_solution(9967036144005209690)
XLA Ops:
  6.5 1.1 slice_bitcast_fusion.99
  7.6 3.7 collective-permute-start
  11.4 1.9 collective-permute-start.1
  13.3 1.0 slice_bitcast_fusion.157
  14.3 4.6 collective-permute-done.1
  18.9 2.0 fusion.118
  20.9 4.9 fusion.53
  26.0 1.6 broadcast_in_dim.24
  27.6 2.1 reshape.317
  29.8 0.1 constant_dynamic-update-slice_fusion.47
  29.9 0.1 constant_dynamic-update-slice_fusion.46
  30.0 0.1 constant_dynamic-update-slice_fusion.45
  30.1 0.1 constant_dynamic-update-slice_fusion.44
  30.2 0.1 constant_dynamic-update-slice_fusion.43
  30.4 0.1 constant_dynamic-update-slice_fusion.42
  30.6 0.1 constant_dynamic-update-slice_fusion.40
  30.7 0.1 constant_dynamic-update-slice_fusion.39
  30.8 0.1 constant_dynamic-update-slice_fusion.38
  30.9 0.1 constant_dynamic-update-slice_fusion.37
  31.0 0.1 constant_dynamic-update-slice_fusion.36
  31.2 0.1 constant_dynamic-update-slice_fusion.35
  31.4 0.1 constant_dynamic-update-slice_fusion.33
  31.5 0.1 constant_dynamic-update-slice_fusion.32
  31.6 0.1 constant_dynamic-update-slice_fusion.31
  31.7 0.1 constant_dynamic-update-slice_fusion.30
  31.8 0.1 constant_dynamic-update-slice_fusion.29
  32.0 0.1 constant_dynamic-update-slice_fusion.28
  32.2 0.1 constant_dynamic-update-slice_fusion.26
  32.3 0.1 constant_dynamic-update-slice_fusion.25
  32.4 0.1 constant_dynamic-update-slice_fusion.23
  32.5 0.1 constant_dynamic-update-slice_fusion.22
  32.9 0.1 constant_dynamic-update-slice_fusion.19
  33.7 0.1 constant_dynamic-update-slice_fusion.12
  34.1 175.5 %all-gather.3.cloned.1.call-done = bf16[12,640,1024]{2,1,0:T(8,128)(2,1)} async-done(((bf16[12,640,128]{2,1,0:T(8,128)(2,1)}), bf16[12,640,1024]{2,1,0:T(8,128)(2,1)}) %all-gather.3.cloned.1.call-update) | async-done | bytes 15728656 | tf_op jit(solution)/shard_map/all_gather | solution.py:110
  209.7 11.8 %convert_bitcast_fusion = bf16[3,12,640,128]{3,2,0,1:T(8,128)(2,1)S(1)} fusion(bf16[12,640,1024]{2,1,0:T(8,128)(2,1)} %all-gather.3.cloned.1.call-done, bf16[3,1024,128]{2,1,0:T(8,128)(2,1)S(1)} %copy-done), kind=kOutput, calls=%fused_computation.54 | convolution fusion | flops 6042746880 | bytes 22413312 | tf_op jit(solution)/shard_map/rck,tkh->trch/dot_general | solution.py:108
  221.5 1.4 fusion.172
  222.9 5.0 collective-permute-start.2
  227.8 1.9 collective-permute-start.3
  229.8 0.1 constant_dynamic-update-slice_fusion.8
  229.9 0.1 constant_dynamic-update-slice_fusion.7
  230.1 0.1 constant_dynamic-update-slice_fusion.5
  230.3 0.1 constant_dynamic-update-slice_fusion.3
  230.6 0.1 constant_dynamic-update-slice_fusion.1
  230.8 2.2 slice.898
  233.0 1.4 slice.896
  234.4 3.2 copy.450
  237.7 10.1 %collective-permute-done.2 = bf16[2,3,640,128]{3,2,0,1:T(8,128)(2,1)} collective-permute-done((bf16[2,3,640,128]{3,2,0,1:T(8,128)(2,1)}, bf16[2,3,640,128]{3,2,0,1:T(8,128)(2,1)}, u32[]{:S(2)}, u32[]{:S(2)}) %collective-permute-start.2) | collective-permute-done | bytes 983072 | tf_op jit(solution)/shard_map/ppermute | solution.py:15
  247.8 2.7 collective-permute-done.3
  250.4 6.3 %pad_maximum_fusion = bf16[2,18,640,128]{3,2,0,1:T(8,128)(2,1)} fusion(bf16[2,3,640,128]{3,2,0,1:T(8,128)(2,1)} %collective-permute-done.3, bf16[2,12,640,128]{3,2,0,1:T(8,128)(2,1)} %slice.898, bf16[2,3,640,128]{3,2,0,1:T(8,128)(2,1)} %collective-permute-done.2), kind=kLoop, calls=%fused_computation.53 | loop fusion | flops 5898240 | bytes 11796480 | tf_op jit(solution)/shard_map/concatenate | solution.py:33
  256.7 8.8 %copy.451 = bf16[2,18,640,128]{2,3,1,0:T(8,128)(2,1)} copy(bf16[2,18,640,128]{3,2,0,1:T(8,128)(2,1)} %pad_maximum_fusion) | data formatting | bytes 11796480
  265.5 6.9 %pad.14.clone = bf16[2,18,646,128]{2,3,1,0:T(8,128)(2,1)S(1)} pad(bf16[2,18,640,128]{2,3,1,0:T(8,128)(2,1)} %copy.451, bf16[]{:T(256)} %constant.9.clone.1), padding=0_0x0_0x3_3x0_0 | pad | bytes 11851778 | tf_op jit(solution)/shard_map/jit(_pad)/pad | solution.py:36
  272.5 14.3 %fusion.51 = (f32[2,12,640]{2,0,1:T(2,128)S(1)}, f32[2,12,640]{2,0,1:T(2,128)S(1)}, f32[2,12,640]{2,0,1:T(2,128)S(1)}, f32[2,12,640]{2,0,1:T(2,128)S(1)}, f32[2,...) fusion(bf16[2,12,640,64]{2,3,0,1:T(8,128)(2,1)S(1)} %bitcast.12, ...), kind=kLoop, calls=%fused_computation.104 | loop fusion | flops 53790720 | bytes 38461440 | tf_op jit(solution)/shard_map/rchd,rchd->hrc/dot_general | solution.py:68
  286.8 9.5 %fusion.49 = (f32[2,12,640]{2,0,1:T(2,128)S(1)}, f32[2,12,640]{2,0,1:T(2,128)S(1)}, f32[2,12,640]{2,0,1:T(2,128)S(1)}, f32[2,12,640]{2,0,1:T(2,128)S(1)}, f32[2,...) fusion(bf16[2,12,640,64]{2,3,0,1:T(8,128)(2,1)S(1)} %bitcast.12, ...), kind=kLoop, calls=%fused_computation.102 | loop fusion | flops 39121920 | bytes 28323840 | tf_op jit(solution)/shard_map/rchd,rchd->hrc/dot_general | solution.py:68
  296.3 14.4 %fusion.50 = (f32[2,12,640]{2,0,1:T(2,128)S(1)}, f32[2,12,640]{2,0,1:T(2,128)S(1)}, f32[2,12,640]{2,0,1:T(2,128)S(1)}, f32[2,12,640]{2,0,1:T(2,128)S(1)}, f32[2,...) fusion(bf16[2,12,640,64]{2,3,0,1:T(8,128)(2,1)S(1)} %bitcast.12, ...), kind=kLoop, calls=%fused_computation.103 | loop fusion | flops 53790720 | bytes 38461440 | tf_op jit(solution)/shard_map/rchd,rchd->hrc/dot_general | solution.py:68
  312.8 2.3 fusion.119
  315.2 3.6 fusion.122
  318.8 3.6 divide_convert_fusion
  322.4 0.4 convert_bitcast_fusion.49
  322.8 0.4 convert_bitcast_fusion.48
  323.2 0.2 convert_bitcast_fusion.47
  323.4 32.4 %fusion.63 = bf16[12,640,2,64]{1,3,2,0:T(8,128)(2,1)S(1)} fusion(bf16[2,18,646,2,64]{2,4,3,1,0:T(8,128)(2,1)S(1)} %bitcast.1272, f32[12,640,2]{1,2,0:T(2,128)S(1)} %get-tuple-element.59, f32[12,640,2]{1,2,0:T(2,128)S(1)} %get-tuple-element.60, f32[12,640,2]{1,2,0:T(2,128)S(1)} %get-tuple-element.61, f32[12,640,2]{1,2,0:T(2,128)S(1)} %get-tuple-element.62, ...), kind=kLoop, calls=%fused_computation.125 | loop fusion | flops 144506880 | bytes 101314560 | tf_op jit(solution)/shard_map/convert_element_type | solution.py:93
  355.8 2.5 copy.56
  358.3 180.1 %all-gather.5.cloned.1.call-done = bf16[12,640,1024]{2,1,0:T(8,128)(2,1)} async-done(((bf16[12,640,128]{2,1,0:T(8,128)(2,1)}), bf16[12,640,1024]{2,1,0:T(8,128)(2,1)}) %all-gather.5.cloned.1.call-update) | async-done | bytes 15728656 | tf_op jit(solution)/shard_map/all_gather | solution.py:120
  538.4 11.6 %fusion.120 = bf16[1,12,640,128]{3,2,1,0:T(8,128)(2,1)} fusion(bf16[12,640,1024]{2,1,0:T(8,128)(2,1)} %all-gather.5.cloned.1.call-done, bf16[1024,128]{1,0:T(8,128)(2,1)S(1)} %copy-done.3, bf16[1,12,640,128]{3,2,1,0:T(8,128)(2,1)} %param.5), kind=kOutput, calls=%fused_computation.232 | convolution fusion | flops 2016215040 | bytes 19922944 | tf_op jit(solution)/shard_map/rck,kh->rch/dot_general | solution.py:118
  (82 shorter events, 3.9 us)
Async XLA Ops:
  6.5 203.1 %copy-start = (bf16[3,1024,128]{2,1,0:T(8,128)(2,1)S(1)}, bf16[3,1024,128]{2,1,0:T(8,128)(2,1)}, u32[]{:S(2)}) copy-start(bf16[3,1024,128]{2,1,0:T(8,128)(2,1)} %param.7) | copy-start | bytes 2359300
  6.5 203.1 %all-gather.3.cloned.1.call-start = ((), (), s32[]{:S(2)}) async-start(), calls=%async_computation | async-start | bytes 17694720 | tf_op jit(solution)/shard_map/all_gather | solution.py:110
  7.6 6.7 %collective-permute-start = (bf16[1,640,128]{2,1,0:T(8,128)(2,1)S(1)}, bf16[1,640,128]{2,1,0:T(8,128)(2,1)S(1)}, u32[]{:S(2)}, u32[]{:S(2)}) collective-permute-start(bf16[1,640,128]{2,1,0:T(8,128)(2,1)S(1)} %get-tuple-element.56), channel_id=1, source_target_pairs={{0,8},{8,16},{16,24},{24,32},{32,40},{40,48},{48,56},{56,64},{64,7... | collective-permute-start | bytes 491528 | tf_op jit(solution)/shard_map/ppermute | solution.py:15
  11.4 7.5 %collective-permute-start.1 = (bf16[1,640,128]{2,1,0:T(8,128)(2,1)S(1)}, bf16[1,640,128]{2,1,0:T(8,128)(2,1)S(1)}, u32[]{:S(2)}, u32[]{:S(2)}) collective-permute-start(bf16[1,640,128]{2,1,0:T(8,128)(2,1)S(1)} %get-tuple-element.57), channel_id=1, source_target_pairs={{8,0},{16,8},{24,16},{32,24},{40,32},{48,40},{56,48},{64,56},{72,6... | collective-permute-start | bytes 491528 | tf_op jit(solution)/shard_map/ppermute | solution.py:15
  20.9 5.0 copy-start.2
  25.9 512.5 %all-gather.5.cloned.1.call-start = ((), (), s32[]{:S(2)}) async-start(), calls=%async_computation.1 | async-start | bytes 17694720 | tf_op jit(solution)/shard_map/all_gather | solution.py:120
  222.9 24.9 %collective-permute-start.2 = (bf16[2,3,640,128]{3,2,0,1:T(8,128)(2,1)}, bf16[2,3,640,128]{3,2,0,1:T(8,128)(2,1)}, u32[]{:S(2)}, u32[]{:S(2)}) collective-permute-start(bf16[2,3,640,128]{3,2,0,1:T(8,128)(2,1)} %get-tuple-element.54), channel_id=1, source_target_pairs={{0,8},{8,16},{16,24},{24,32},{32,40},{40,48},{48,56},{56,64},{64,7... | collective-permute-start | bytes 2949128 | tf_op jit(solution)/shard_map/ppermute | solution.py:15
  227.8 22.6 %collective-permute-start.3 = (bf16[2,3,640,128]{3,2,0,1:T(8,128)(2,1)}, bf16[2,3,640,128]{3,2,0,1:T(8,128)(2,1)}, u32[]{:S(2)}, u32[]{:S(2)}) collective-permute-start(bf16[2,3,640,128]{3,2,0,1:T(8,128)(2,1)} %get-tuple-element.55), channel_id=1, source_target_pairs={{8,0},{16,8},{24,16},{32,24},{40,32},{48,40},{56,48},{64,56},{72,6... | collective-permute-start | bytes 2949128 | tf_op jit(solution)/shard_map/ppermute | solution.py:15
  355.8 182.6 %copy-start.3 = (bf16[1024,128]{1,0:T(8,128)(2,1)S(1)}, bf16[1024,128]{1,0:T(8,128)(2,1)}, u32[]{:S(2)}) copy-start(bf16[1024,128]{1,0:T(8,128)(2,1)} %param.8) | copy-start | bytes 786436
  538.4 11.6 %copy-start.1 = (bf16[3,1024,128]{2,1,0:T(8,128)(2,1)S(1)}, bf16[3,1024,128]{2,1,0:T(8,128)(2,1)}, u32[]{:S(2)}) copy-start(bf16[3,1024,128]{2,1,0:T(8,128)(2,1)} %param.7) | copy-start | bytes 2359300
Sparse Core Ops, SparseCore 0:
  26.0 183.6 all-gather.2
  358.5 179.9 all-gather.4
where the time goes:
time: 568 us; the launch traced here: 557 us
  waiting for transfers between devices  373 us (66%)
  other arithmetic  102 us (18%)
  local copies, waits for them, and re-layouts  32.3 us (6%)
  matrix products  23.4 us (4%)
  between operations  14.2 us (2%)
  starting transfers between devices  12.6 us (2%)
    all_gather x1, waiting for transfers between devices, per_device(): lax.all_gather(attended, 'head', axis=2, tiled=True)  180 us
    all_gather x1, waiting for transfers between devices, per_device(): lax.all_gather(mixed, 'head', axis=2, tiled=True)  176 us
    dot_general x3, other arithmetic, attend(): jnp.einsum('rchd,rchd->hrc', query_parts, key_part, preferred_element_typ...  38.2 us
    convert_element_type x1, other arithmetic, attend(): running.reshape(row_count, col_count, chan_count).astype(jnp.bfloat16)  32.4 us
    ppermute x4, waiting for transfers between devices, passed_along(): return lax.ppermute(block, axis, route)  17.4 us
    ppermute x4, starting transfers between devices, passed_along(): return lax.ppermute(block, axis, route)  12.5 us
    unnamed x11, local copies, waits for them, and re-layouts  12.1 us
    dot_general x1, matrix products, per_device(): jnp.einsum('rck,tkh->trch', lax.all_gather(mixed, 'head', axis=2, tiled=T...  11.8 us
  transfers between devices with their start and end apart: 6, of which 5 were waited for; matrix products, arithmetic and copies ran while one was open for 3% of the time, Pallas kernels for 0%

commit v1 on v0

v1 whole, which is shorter than its diff:
```python
import functools
import math

import jax
import jax.numpy as jnp
from jax import lax
from jax.experimental import pallas as pl
from jax.experimental.pallas import tpu as pltpu
from jax.sharding import PartitionSpec as P

MESH = pl.DeviceIdType.MESH
NT = 16
NH = 8
ROWS = 12
COLS = 640
CW = 80
WC = 96
BC = 112
CH = 128
D = 1024
TILE = 32
WROWS = ROWS + 8
KROWS = ROWS + 6
SLAB = 128
NEG = -1e30
EXP_SCALE = math.log2(math.e) / 8.0


def kernel(
    cells, conv_w, wqkv, wout, bmask, out,
    win, w4, cw, mixed, qbuf, kbuf, vbuf, att, ob,
    loc_sem, w_s, w_r, o_s, o_r, c_s, c_r, m_s, m_r, u_s, u_r, d_s, d_r,
    y_s, y_r, r_s, r_r, rl_s,
):
    t = lax.axis_index("tile")
    h = lax.axis_index("head")
    yrow = t // 4
    core = t % 2
    low = (t // 2) % 2
    y_up = (t + 4) % NT
    y_dn = (t + 12) % NT
    sib = t + 1 - 2 * core
    not_top = t > 0
    not_bot = t < NT - 1

    def slab_row(yy, cc):
        return pl.multiple_of(SLAB * (2 * yy + cc), SLAB)

    @pl.when(t == 0)
    def _():
        win[:, 0:4] = jnp.zeros((NH, 4, BC, CH), jnp.bfloat16)

    @pl.when(t == NT - 1)
    def _():
        win[:, 16:20] = jnp.zeros((NH, 4, BC, CH), jnp.bfloat16)

    @pl.when(h == 0)
    def _():
        win[:, :, 0:16] = jnp.zeros((NH, WROWS, 16, CH), jnp.bfloat16)

    @pl.when(h == NH - 1)
    def _():
        win[:, :, 96:112] = jnp.zeros((NH, WROWS, 16, CH), jnp.bfloat16)

    bar = pltpu.get_barrier_semaphore()
    for k in range(1, NH):
        pl.semaphore_signal(bar, inc=1, device_id=(t, (h + k) % NH), device_id_type=MESH)
    for other in (y_up, y_dn):
        pl.semaphore_signal(bar, inc=1, device_id=(other, h), device_id_type=MESH)

    @pl.when(not_top)
    def _():
        for k in range(NH):
            pl.semaphore_signal(bar, inc=1, device_id=(t - 1, (h + k) % NH), device_id_type=MESH)

    @pl.when(not_bot)
    def _():
        for k in range(NH):
            pl.semaphore_signal(bar, inc=1, device_id=(t + 1, (h + k) % NH), device_id_type=MESH)

    bands_near = jnp.where(not_top, 1, 0) + jnp.where(not_bot, 1, 0)
    pl.semaphore_wait(bar, NH + 1 + NH * bands_near)

    def win_start(hd):
        return pl.multiple_of(jnp.clip(CW * hd - 8, 0, COLS - WC), 8)

    def win_at(hd):
        return pl.multiple_of(win_start(hd) - CW * hd + 16, 8)

    own_rows = slab_row(yrow, core)

    def w_copy(k, hs, ht):
        return pltpu.make_async_remote_copy(
            src_ref=wqkv.at[:, pl.ds(own_rows, SLAB), :],
            dst_ref=w4.at[0:3, pl.ds(own_rows, SLAB), pl.ds(pl.multiple_of(CH * hs, CH), CH)],
            send_sem=w_s.at[k], recv_sem=w_r.at[k],
            device_id=(t, ht), device_id_type=MESH)

    def o_copy(k, hs, ht):
        return pltpu.make_async_remote_copy(
            src_ref=wout.at[pl.ds(own_rows, SLAB), :],
            dst_ref=w4.at[3, pl.ds(own_rows, SLAB), pl.ds(pl.multiple_of(CH * hs, CH), CH)],
            send_sem=o_s.at[k], recv_sem=o_r.at[k],
            device_id=(t, ht), device_id_type=MESH)

    def c_copy(k, hs, ht):
        return pltpu.make_async_remote_copy(
            src_ref=conv_w, dst_ref=cw.at[hs],
            send_sem=c_s.at[k], recv_sem=c_r.at[k],
            device_id=(t, ht), device_id_type=MESH)

    def m_copy(k, hs, ht):
        return pltpu.make_async_remote_copy(
            src_ref=cells.at[0, :, pl.ds(win_start(ht), WC), :],
            dst_ref=win.at[hs, 4:16, pl.ds(win_at(ht), WC), :],
            send_sem=m_s.at[k], recv_sem=m_r.at[k],
            device_id=(t, ht), device_id_type=MESH)

    def u_copy(k, hs, ht):
        return pltpu.make_async_remote_copy(
            src_ref=cells.at[0, 0:4, pl.ds(win_start(ht), WC), :],
            dst_ref=win.at[hs, 16:20, pl.ds(win_at(ht), WC), :],
            send_sem=u_s.at[k], recv_sem=u_r.at[k],
            device_id=(t - 1, ht), device_id_type=MESH)

    def d_copy(k, hs, ht):
        return pltpu.make_async_remote_copy(
            src_ref=cells.at[0, 8:12, pl.ds(win_start(ht), WC), :],
            dst_ref=win.at[hs, 0:4, pl.ds(win_at(ht), WC), :],
            send_sem=d_s.at[k], recv_sem=d_r.at[k],
            device_id=(t + 1, ht), device_id_type=MESH)

    local = [
        pltpu.make_async_copy(
            wqkv.at[:, pl.ds(own_rows, SLAB), :],
            w4.at[0:3, pl.ds(own_rows, SLAB), pl.ds(pl.multiple_of(CH * h, CH), CH)], loc_sem.at[0]),
        pltpu.make_async_copy(
            wout.at[pl.ds(own_rows, SLAB), :],
            w4.at[3, pl.ds(own_rows, SLAB), pl.ds(pl.multiple_of(CH * h, CH), CH)], loc_sem.at[1]),
        pltpu.make_async_copy(conv_w, cw.at[h], loc_sem.at[2]),
        pltpu.make_async_copy(
            cells.at[0, :, pl.ds(win_start(h), WC), :],
            win.at[h, 4:16, pl.ds(win_at(h), WC), :], loc_sem.at[3]),
    ]
    for k in range(1, NH):
        ht = (h + k) % NH
        w_copy(k, h, ht).start()
        o_copy(k, h, ht).start()
    for cp in local:
        cp.start()
    for k in range(1, NH):
        c_copy(k, h, (h + k) % NH).start()
    for k in range(NH):
        ht = (h + k) % NH
        if k:
            m_copy(k, h, ht).start()

        @pl.when(not_top)
        def _():
            u_copy(k, h, ht).start()

        @pl.when(not_bot)
        def _():
            d_copy(k, h, ht).start()

    def y_copy(idx, yy, cc, to, first=0, size=SLAB):
        rows = pl.ds(pl.multiple_of(slab_row(yy, cc) + first, size), size)
        return pltpu.make_async_remote_copy(
            src_ref=w4.at[:, rows, :], dst_ref=w4.at[:, rows, :],
            send_sem=y_s.at[idx], recv_sem=y_r.at[idx],
            device_id=(to, h), device_id_type=MESH)

    y1 = (yrow + 3) % 4
    y2 = (yrow + 2) % 4
    y3 = (yrow + 1) % 4
    other = 1 - core
    half = SLAB // 2

    local[0].wait()
    local[1].wait()
    for k in range(1, NH):
        hs = (h + NH - k) % NH
        w_copy(k, hs, h).wait_recv()
        o_copy(k, hs, h).wait_recv()
    y_copy(0, yrow, core, y_up).start()
    y_copy(1, yrow, core, y_dn).start()
    y_copy(2, yrow, core, sib).start()

    y_copy(0, y1, core, y_up).wait_recv()
    y_copy(3, y1, core, y_up, 0, half).start()
    y_copy(5, y1, core, sib).start()
    y_copy(1, y3, core, y_dn).wait_recv()
    y_copy(4, y3, core, y_dn, half, half).start()
    y_copy(6, y3, core, sib).start()

    local[2].wait()
    local[3].wait()

    def conv_chunk(k, carry):
        hs = (h + NH - k) % NH

        @pl.when(k > 0)
        def _():
            c_copy(k, hs, h).wait_recv()
            m_copy(k, hs, h).wait_recv()

        @pl.when(not_bot)
        def _():
            u_copy(k, hs, h).wait_recv()

        @pl.when(not_top)
        def _():
            d_copy(k, hs, h).wait_recv()

        taps = [jnp.broadcast_to(cw[hs, pl.ds(i, 1), :], (WC, CH)) for i in range(9)]
        lanes = pl.ds(pl.multiple_of(CH * hs, CH), CH)

        def row(i):
            return win[hs, i].astype(jnp.float32)[8:104]

        rows = [row(0), row(1), None]
        for r in range(KROWS):
            rows[2] = row(r + 2)
            side = []
            for b in range(3):
                acc = taps[b] * rows[0]
                acc = acc + taps[3 + b] * rows[1]
                acc = acc + taps[6 + b] * rows[2]
                side.append(acc)
            conv = pltpu.roll(side[0], 1, 0) + side[1] + pltpu.roll(side[2], WC - 1, 0)
            mixed[pl.ds(WC * r, WC), lanes] = (rows[1] + conv).astype(jnp.bfloat16)
            rows = [rows[1], rows[2], None]
        return carry

    lax.fori_loop(0, 4, conv_chunk, 0)

    y_copy(3, y2, core, y_up, 0, half).wait_recv()
    y_copy(4, y2, core, y_dn, half, half).wait_recv()
    y_copy(7, y2, core, sib).start()

    lax.fori_loop(4, NH, conv_chunk, 0)

    y_copy(2, yrow, other, sib).wait_recv()
    y_copy(5, y1, other, sib).wait_recv()
    y_copy(6, y3, other, sib).wait_recv()
    y_copy(7, y2, other, sib).wait_recv()

    BLK = 3 * WC

    def kv_block(i, carry):
        def part(n, c2):
            lanes = pl.ds(pl.multiple_of(256 * n, 256), 256)
            x = mixed[pl.ds(pl.multiple_of(BLK * i, BLK), BLK), :]
            for plane, ref in ((1, kbuf), (2, vbuf)):
                y = jnp.dot(x, w4[plane, :, lanes], preferred_element_type=jnp.float32)
                ref[pl.ds(3 * i, 3), :, lanes] = y.astype(jnp.bfloat16).reshape(3, WC, 256)
            return c2

        return lax.fori_loop(0, 4, part, carry)

    def q_block(i, carry):
        def part(n, c2):
            lanes = pl.ds(pl.multiple_of(256 * n, 256), 256)
            x = mixed[pl.ds(pl.multiple_of(BLK * (i + 1), BLK), BLK), :]
            y = jnp.dot(x, w4[0, :, lanes], preferred_element_type=jnp.float32)
            y = y.reshape(3, WC, 256)[:, 8:88]
            qbuf[pl.ds(3 * i, 3), :, lanes] = y.astype(jnp.bfloat16)
            return c2

        return lax.fori_loop(0, 4, part, carry)

    lax.fori_loop(0, 6, kv_block, 0)
    lax.fori_loop(0, 4, q_block, 0)

    qi = lax.broadcasted_iota(jnp.int32, (32, 256), 0)
    ki = lax.broadcasted_iota(jnp.int32, (32, 256), 1)
    drow = ki // 32 - qi // 16 - 3
    dcol = ki % 32 - qi % 16 - 8
    band = (drow >= -3) & (drow <= 3) & (dcol >= -3) & (dcol <= 3)
    self_bias = jnp.where((drow == 0) & (dcol == 0), 0.0, NEG).astype(jnp.float32)
    band_f = jnp.where(band, 1.0, 0.0).astype(jnp.float32)
    lane1 = lax.broadcasted_iota(jnp.int32, (1, 256), 1)
    head_of = lax.broadcasted_iota(jnp.int32, (32, 256), 1) // 64
    head_on = [jnp.where(head_of == i, 1.0, 0.0).astype(jnp.bfloat16) for i in range(4)]

    def occ_at(rt, ct):
        inside = (rt >= 0) & (rt < 6) & (ct >= 0) & (ct < 20)
        value = bmask[jnp.clip(rt, 0, 5), jnp.clip(ct, 0, 19)]
        return jnp.where(inside, value, 0)

    def r_copy(i, k, hs, ht):
        return pltpu.make_async_remote_copy(
            src_ref=ob.at[ht, pl.ds(2 * i, 2)],
            dst_ref=out.at[0, pl.ds(2 * i, 2), pl.ds(pl.multiple_of(CW * hs, 16), CW), :],
            send_sem=r_s.at[i, k], recv_sem=r_r.at[i, k],
            device_id=(t, ht), device_id_type=MESH)

    def r_local(i):
        return pltpu.make_async_copy(
            ob.at[h, pl.ds(2 * i, 2)],
            out.at[0, pl.ds(2 * i, 2), pl.ds(pl.multiple_of(CW * h, 16), CW), :],
            rl_s.at[i])

    def row_pair(i, carry):
        r0 = 2 * i

        def col_tile(j, c2):
            row0 = ROWS * t - 3 + r0
            col0 = CW * h - 8 + 16 * j
            rt = (row0 + 32) // 32 - 1
            ct = (col0 + 32) // 32 - 1
            in_r = (row0 + lane1 // 32 + 32) // 32 - 1 == rt
            in_c = (col0 + lane1 % 32 + 32) // 32 - 1 == ct
            occ = jnp.where(
                in_r,
                jnp.where(in_c, occ_at(rt, ct), occ_at(rt, ct + 1)),
                jnp.where(in_c, occ_at(rt + 1, ct), occ_at(rt + 1, ct + 1)))
            occ_f = occ.astype(jnp.float32)
            bias = jnp.where(band_f * occ_f > 0.5, 0.0, self_bias)
            cols = pl.ds(pl.multiple_of(16 * j, 16), 16)
            kcols = pl.ds(pl.multiple_of(16 * j, 16), 32)
            for g in range(4):
                lanes = slice(256 * g, 256 * g + 256)
                q = qbuf[pl.ds(r0, 2), cols, lanes].reshape(32, 256)
                kk = kbuf[pl.ds(r0, 8), kcols, lanes].reshape(256, 256)
                vv = vbuf[pl.ds(r0, 8), kcols, lanes].reshape(256, 256)
                q4 = jnp.concatenate([q * head_on[n] for n in range(4)], axis=0)
                s = lax.dot_general(q4, kk, (((1,), (1,)), ((), ())),
                                    preferred_element_type=jnp.float32)
                s = s.reshape(4, 32, 256) + bias[None]
                peak = jnp.max(s, axis=-1, keepdims=True)
                e = jnp.exp2((s - peak) * EXP_SCALE)
                total = jnp.sum(e, axis=-1, keepdims=True)
                p = (e * (1.0 / total)).astype(jnp.bfloat16).reshape(128, 256)
                o = jnp.dot(p, vv, preferred_element_type=jnp.float32)
                o = jnp.where(
                    head_of == 0, o[0:32],
                    jnp.where(head_of == 1, o[32:64],
                              jnp.where(head_of == 2, o[64:96], o[96:128])))
                att[:, cols, lanes] = o.astype(jnp.bfloat16).reshape(2, 16, 256)
            return c2

        lax.fori_loop(0, 5, col_tile, 0)

        x = att[...].reshape(2 * CW, D)
        for n in range(4):
            y = jnp.dot(x, w4[3, :, 256 * n:256 * n + 256], preferred_element_type=jnp.float32)
            for m in range(2):
                dst = 2 * n + m
                slab = win[dst, pl.ds(4 + r0, 2), 16:96, :].astype(jnp.float32)
                res = slab + y[:, CH * m:CH * m + CH].reshape(2, CW, CH)
                ob[dst, pl.ds(r0, 2)] = res.astype(jnp.bfloat16)
        r_local(i).start()
        for k in range(1, NH):
            r_copy(i, k, h, (h + k) % NH).start()
        return carry

    lax.fori_loop(0, ROWS // 2, row_pair, 0)

    def drain(i, carry):
        r_local(i).wait()
        for k in range(1, NH):
            r_copy(i, k, h, (h + k) % NH).wait_send()
            r_copy(i, k, (h + NH - k) % NH, h).wait_recv()
        return carry

    for k in range(1, NH):
        ht = (h + k) % NH
        w_copy(k, h, ht).wait_send()
        o_copy(k, h, ht).wait_send()
        c_copy(k, h, ht).wait_send()
        m_copy(k, h, ht).wait_send()
    for k in range(NH):
        ht = (h + k) % NH

        @pl.when(not_top)
        def _():
            u_copy(k, h, ht).wait_send()

        @pl.when(not_bot)
        def _():
            d_copy(k, h, ht).wait_send()
    y_copy(0, yrow, core, y_up).wait_send()
    y_copy(1, yrow, core, y_dn).wait_send()
    y_copy(2, yrow, core, sib).wait_send()
    y_copy(3, y1, core, y_up, 0, half).wait_send()
    y_copy(4, y3, core, y_dn, half, half).wait_send()
    y_copy(5, y1, core, sib).wait_send()
    y_copy(6, y3, core, sib).wait_send()
    y_copy(7, y2, core, sib).wait_send()
    lax.fori_loop(0, ROWS // 2, drain, 0)


def per_device(cells, conv_weight, qkv_weight, out_weight, block_mask):
    hbm = pl.BlockSpec(memory_space=pl.ANY)
    bf = jnp.bfloat16
    sem = pltpu.SemaphoreType.DMA
    pairs = ROWS // 2
    return pl.pallas_call(
        kernel,
        out_shape=jax.ShapeDtypeStruct((1, ROWS, COLS, CH), bf),
        in_specs=[hbm, hbm, hbm, hbm, pl.BlockSpec(memory_space=pltpu.SMEM)],
        out_specs=hbm,
        scratch_shapes=[
            pltpu.VMEM((NH, WROWS, BC, CH), bf),
            pltpu.VMEM((4, D, D), bf),
            pltpu.VMEM((NH, 9, CH), jnp.float32),
            pltpu.VMEM((KROWS * WC, D), bf),
            pltpu.VMEM((ROWS, CW, D), bf),
            pltpu.VMEM((KROWS, WC, D), bf),
            pltpu.VMEM((KROWS, WC, D), bf),
            pltpu.VMEM((2, CW, D), bf),
            pltpu.VMEM((NH, ROWS, CW, CH), bf),
            sem((4,)),
            sem((NH,)), sem((NH,)), sem((NH,)), sem((NH,)), sem((NH,)), sem((NH,)),
            sem((NH,)), sem((NH,)), sem((NH,)), sem((NH,)), sem((NH,)), sem((NH,)),
            sem((8,)), sem((8,)),
            sem((pairs, NH)), sem((pairs, NH)), sem((pairs,)),
        ],
        compiler_params=pltpu.CompilerParams(
            collective_id=0, has_side_effects=True, vmem_limit_bytes=56 * 1024 * 1024),
        name="band_layer",
    )(cells, conv_weight, qkv_weight, out_weight, block_mask)


def solution(mesh):
    placed = (
        P("tile", None, None, "head"),
        P(None, "head"),
        P(None, None, "head"),
        P(None, "head"),
        P(),
    )
    return jax.shard_map(
        per_device,
        mesh=mesh,
        in_specs=placed,
        out_specs=P("tile", None, None, "head"),
        check_vma=False,
    )
```

time: 568 us -> 166 us (0.29); the launches traced: 557 us -> 163 us
  waiting for transfers between devices: 373 us -> 0 us
  Pallas kernels: 0 us -> 160 us
  other arithmetic: 102 us -> 0 us
  local copies, waits for them, and re-layouts: 32.3 us -> 2.94 us
  matrix products: 23.4 us -> 0 us
  between operations: 14.2 us -> 0.01 us
  starting transfers between devices: 12.6 us -> 0 us
    all_gather x2 -> x0, waiting for transfers between devices: 356 us -> none  [the longest x1 180 us: per_device(): lax.all_gather(attended, 'head', axis=2, tiled=True)]
    pallas_call x0 -> x1, Pallas kernels: none -> 160 us  [per_device(): pl.pallas_call(kernel, out_shape=jax.ShapeDtypeStruct((1, ROWS, COLS, CH)...]
    convert_element_type x4 -> x0, other arithmetic: 42.9 us -> none  [the longest x1 32.4 us: attend(): running.reshape(row_count, col_count, chan_count).astype(jnp.bfloat16)]
    dot_general x3 -> x0, other arithmetic: 38.2 us -> none  [attend(): jnp.einsum('rchd,rchd->hrc', query_parts, key_part, preferred_element_typ...]
    dot_general x2 -> x0, matrix products: 23.4 us -> none  [the longest x1 11.8 us: per_device(): jnp.einsum('rck,tkh->trch', lax.all_gather(mixed, 'head', axis=2, tiled=T...]
    ppermute x4 -> x0, waiting for transfers between devices: 17.4 us -> none  [passed_along(): return lax.ppermute(block, axis, route)]
    ppermute x4 -> x0, starting transfers between devices: 12.5 us -> none  [passed_along(): return lax.ppermute(block, axis, route)]
    unnamed x11 -> x1, local copies, waits for them, and re-layouts: 12.1 us -> 2.94 us
  transfers between devices with their start and end apart: 6 -> 0, of which waited for: 5 -> 0; matrix products, arithmetic and copies ran while one was open for 3% -> 0% of each run, Pallas kernels for 0% -> 0%
where the time goes in v1:
time: 166 us; the launch traced here: 163 us
  Pallas kernels  160 us (96%)
  local copies, waits for them, and re-layouts  2.94 us (2%)
    pallas_call x1, Pallas kernels, per_device(): pl.pallas_call(kernel, out_shape=jax.ShapeDtypeStruct((1, ROWS, COLS, CH)...  160 us

profile of v1, /device:TPU:3, one launch (start us, length us, event | category | flops | bytes accessed | tf_op | source)
XLA Modules:
  0.0 163.2 jit_solution(9068142518343117417)
XLA Ops:
  0.0 160.2 %band_layer.1 = bf16[1,12,640,128]{3,2,1,0:T(8,128)(2,1)} custom-call(bf16[1,12,640,128]{3,2,1,0:T(8,128)(2,1)} %cells.1, f32[9,128]{1,0:T(8,128)} %conv_w.1, bf16[3,1024,128]{2,1,0:T(8,128)(2,1)} %wqkv.1, bf16[1024,128]{1,0:T(8,128)(2,1)} %wout.1, s32[6,20]{1,0:T(8,128)} %bmask.1), custom_call_target="tpu_custom_call" | custom-call | tf_op jit(solution)/shard_map/band_layer/pallas_call | solution.py:399
  160.2 2.9 %copy.7 = bf16[1,12,640,128]{3,2,1,0:T(8,128)(2,1)} copy(bf16[1,12,640,128]{3,2,1,0:T(8,128)(2,1)} %band_layer.1) | data formatting | bytes 3932160

commit v2 on v1

--- a/solution.py
+++ b/solution.py
@@ -22,6 +22,8 @@
 WROWS = ROWS + 8
 KROWS = ROWS + 6
 SLAB = 128
+AHEAD = 2
+EARLY = 3
 NEG = -1e30
 EXP_SCALE = math.log2(math.e) / 8.0
 
@@ -40,6 +42,7 @@
     y_up = (t + 4) % NT
     y_dn = (t + 12) % NT
     sib = t + 1 - 2 * core
+    flip = 2 - 4 * low
     not_top = t > 0
     not_bot = t < NT - 1
 
@@ -67,19 +70,20 @@
         pl.semaphore_signal(bar, inc=1, device_id=(t, (h + k) % NH), device_id_type=MESH)
     for other in (y_up, y_dn):
         pl.semaphore_signal(bar, inc=1, device_id=(other, h), device_id_type=MESH)
+    for z in range(4):
+        far = 4 * (1 - h // 4) + z
+        pl.semaphore_signal(bar, inc=1, device_id=(t + flip, far), device_id_type=MESH)
 
     @pl.when(not_top)
     def _():
-        for k in range(NH):
-            pl.semaphore_signal(bar, inc=1, device_id=(t - 1, (h + k) % NH), device_id_type=MESH)
+        pl.semaphore_signal(bar, inc=1, device_id=(t - 1, h), device_id_type=MESH)
 
     @pl.when(not_bot)
     def _():
-        for k in range(NH):
-            pl.semaphore_signal(bar, inc=1, device_id=(t + 1, (h + k) % NH), device_id_type=MESH)
+        pl.semaphore_signal(bar, inc=1, device_id=(t + 1, h), device_id_type=MESH)
 
     bands_near = jnp.where(not_top, 1, 0) + jnp.where(not_bot, 1, 0)
-    pl.semaphore_wait(bar, NH + 1 + NH * bands_near)
+    pl.semaphore_wait(bar, NH - 1 + 2 + 4 + bands_near)
 
     def win_start(hd):
         return pl.multiple_of(jnp.clip(CW * hd - 8, 0, COLS - WC), 8)
@@ -88,20 +92,23 @@
         return pl.multiple_of(win_start(hd) - CW * hd + 16, 8)
 
     own_rows = slab_row(yrow, core)
+
+    def tile_for(hs, ht):
+        return t + flip * ((hs // 4 + ht // 4) % 2)
 
     def w_copy(k, hs, ht):
         return pltpu.make_async_remote_copy(
             src_ref=wqkv.at[:, pl.ds(own_rows, SLAB), :],
             dst_ref=w4.at[0:3, pl.ds(own_rows, SLAB), pl.ds(pl.multiple_of(CH * hs, CH), CH)],
             send_sem=w_s.at[k], recv_sem=w_r.at[k],
-            device_id=(t, ht), device_id_type=MESH)
+            device_id=(tile_for(hs, ht), ht), device_id_type=MESH)
 
     def o_copy(k, hs, ht):
         return pltpu.make_async_remote_copy(
             src_ref=wout.at[pl.ds(own_rows, SLAB), :],
             dst_ref=w4.at[3, pl.ds(own_rows, SLAB), pl.ds(pl.multiple_of(CH * hs, CH), CH)],
             send_sem=o_s.at[k], recv_sem=o_r.at[k],
-            device_id=(t, ht), device_id_type=MESH)
+            device_id=(tile_for(hs, ht), ht), device_id_type=MESH)
 
     def c_copy(k, hs, ht):
         return pltpu.make_async_remote_copy(
@@ -116,19 +123,30 @@
             send_sem=m_s.at[k], recv_sem=m_r.at[k],
             device_id=(t, ht), device_id_type=MESH)
 
-    def u_copy(k, hs, ht):
-        return pltpu.make_async_remote_copy(
-            src_ref=cells.at[0, 0:4, pl.ds(win_start(ht), WC), :],
-            dst_ref=win.at[hs, 16:20, pl.ds(win_at(ht), WC), :],
+    own_win = pl.ds(win_at(h), WC)
+
+    def u_copy(k, hs):
+        return pltpu.make_async_remote_copy(
+            src_ref=win.at[hs, 4:8, own_win, :], dst_ref=win.at[hs, 16:20, own_win, :],
             send_sem=u_s.at[k], recv_sem=u_r.at[k],
-            device_id=(t - 1, ht), device_id_type=MESH)
-
-    def d_copy(k, hs, ht):
-        return pltpu.make_async_remote_copy(
-            src_ref=cells.at[0, 8:12, pl.ds(win_start(ht), WC), :],
-            dst_ref=win.at[hs, 0:4, pl.ds(win_at(ht), WC), :],
+            device_id=(t - 1, h), device_id_type=MESH)
+
+    def d_copy(k, hs):
+        return pltpu.make_async_remote_copy(
+            src_ref=win.at[hs, 12:16, own_win, :], dst_ref=win.at[hs, 0:4, own_win, :],
             send_sem=d_s.at[k], recv_sem=d_r.at[k],
-            device_id=(t + 1, ht), device_id_type=MESH)
+            device_id=(t + 1, h), device_id_type=MESH)
+
+    def pass_on(k):
+        hs = (h + NH - k) % NH
+
+        @pl.when(not_top)
+        def _():
+            u_copy(k, hs).start()
+
+        @pl.when(not_bot)
+        def _():
+            d_copy(k, hs).start()
 
     local = [
         pltpu.make_async_copy(
@@ -150,18 +168,10 @@
         cp.start()
     for k in range(1, NH):
         c_copy(k, h, (h + k) % NH).start()
-    for k in range(NH):
-        ht = (h + k) % NH
-        if k:
-            m_copy(k, h, ht).start()
-
-        @pl.when(not_top)
-        def _():
-            u_copy(k, h, ht).start()
-
-        @pl.when(not_bot)
-        def _():
-            d_copy(k, h, ht).start()
+    for k in range(1, NH):
+        m_copy(k, h, (h + k) % NH).start()
+    local[3].wait()
+    pass_on(0)
 
     def y_copy(idx, yy, cc, to, first=0, size=SLAB):
         rows = pl.ds(pl.multiple_of(slab_row(yy, cc) + first, size), size)
@@ -186,31 +196,30 @@
     y_copy(1, yrow, core, y_dn).start()
     y_copy(2, yrow, core, sib).start()
 
-    y_copy(0, y1, core, y_up).wait_recv()
-    y_copy(3, y1, core, y_up, 0, half).start()
-    y_copy(5, y1, core, sib).start()
-    y_copy(1, y3, core, y_dn).wait_recv()
-    y_copy(4, y3, core, y_dn, half, half).start()
-    y_copy(6, y3, core, sib).start()
-
     local[2].wait()
-    local[3].wait()
+    for k in range(1, AHEAD):
+        m_copy(k, (h + NH - k) % NH, h).wait_recv()
+        pass_on(k)
 
     def conv_chunk(k, carry):
         hs = (h + NH - k) % NH
 
+        @pl.when(k + AHEAD < NH)
+        def _():
+            m_copy(k + AHEAD, (hs + NH - AHEAD) % NH, h).wait_recv()
+            pass_on(k + AHEAD)
+
         @pl.when(k > 0)
         def _():
             c_copy(k, hs, h).wait_recv()
-            m_copy(k, hs, h).wait_recv()
 
         @pl.when(not_bot)
         def _():
-            u_copy(k, hs, h).wait_recv()
+            u_copy(k, hs).wait_recv()
 
         @pl.when(not_top)
         def _():
-            d_copy(k, hs, h).wait_recv()
+            d_copy(k, hs).wait_recv()
 
         taps = [jnp.broadcast_to(cw[hs, pl.ds(i, 1), :], (WC, CH)) for i in range(9)]
         lanes = pl.ds(pl.multiple_of(CH * hs, CH), CH)
@@ -232,13 +241,20 @@
             rows = [rows[1], rows[2], None]
         return carry
 
-    lax.fori_loop(0, 4, conv_chunk, 0)
+    lax.fori_loop(0, EARLY, conv_chunk, 0)
+
+    y_copy(0, y1, core, y_up).wait_recv()
+    y_copy(3, y1, core, y_up, 0, half).start()
+    y_copy(5, y1, core, sib).start()
+    y_copy(1, y3, core, y_dn).wait_recv()
+    y_copy(4, y3, core, y_dn, half, half).start()
+    y_copy(6, y3, core, sib).start()
+
+    lax.fori_loop(EARLY, NH, conv_chunk, 0)
 
     y_copy(3, y2, core, y_up, 0, half).wait_recv()
     y_copy(4, y2, core, y_dn, half, half).wait_recv()
     y_copy(7, y2, core, sib).start()
-
-    lax.fori_loop(4, NH, conv_chunk, 0)
 
     y_copy(2, yrow, other, sib).wait_recv()
     y_copy(5, y1, other, sib).wait_recv()
@@ -319,20 +335,24 @@
             bias = jnp.where(band_f * occ_f > 0.5, 0.0, self_bias)
             cols = pl.ds(pl.multiple_of(16 * j, 16), 16)
             kcols = pl.ds(pl.multiple_of(16 * j, 16), 32)
+            scores, probs = [], []
             for g in range(4):
                 lanes = slice(256 * g, 256 * g + 256)
                 q = qbuf[pl.ds(r0, 2), cols, lanes].reshape(32, 256)
                 kk = kbuf[pl.ds(r0, 8), kcols, lanes].reshape(256, 256)
-                vv = vbuf[pl.ds(r0, 8), kcols, lanes].reshape(256, 256)
                 q4 = jnp.concatenate([q * head_on[n] for n in range(4)], axis=0)
-                s = lax.dot_general(q4, kk, (((1,), (1,)), ((), ())),
-                                    preferred_element_type=jnp.float32)
-                s = s.reshape(4, 32, 256) + bias[None]
+                scores.append(lax.dot_general(q4, kk, (((1,), (1,)), ((), ())),
+                                              preferred_element_type=jnp.float32))
+            for g in range(4):
+                s = scores[g].reshape(4, 32, 256) + bias[None]
                 peak = jnp.max(s, axis=-1, keepdims=True)
                 e = jnp.exp2((s - peak) * EXP_SCALE)
                 total = jnp.sum(e, axis=-1, keepdims=True)
-                p = (e * (1.0 / total)).astype(jnp.bfloat16).reshape(128, 256)
-                o = jnp.dot(p, vv, preferred_element_type=jnp.float32)
+                probs.append((e * (1.0 / total)).astype(jnp.bfloat16).reshape(128, 256))
+            for g in range(4):
+                lanes = slice(256 * g, 256 * g + 256)
+                vv = vbuf[pl.ds(r0, 8), kcols, lanes].reshape(256, 256)
+                o = jnp.dot(probs[g], vv, preferred_element_type=jnp.float32)
                 o = jnp.where(
                     head_of == 0, o[0:32],
                     jnp.where(head_of == 1, o[32:64],
@@ -371,15 +391,15 @@
         c_copy(k, h, ht).wait_send()
         m_copy(k, h, ht).wait_send()
     for k in range(NH):
-        ht = (h + k) % NH
+        hs = (h + NH - k) % NH
 
         @pl.when(not_top)
         def _():
-            u_copy(k, h, ht).wait_send()
+            u_copy(k, hs).wait_send()
 
         @pl.when(not_bot)
         def _():
-            d_copy(k, h, ht).wait_send()
+            d_copy(k, hs).wait_send()
     y_copy(0, yrow, core, y_up).wait_send()
     y_copy(1, yrow, core, y_dn).wait_send()
     y_copy(2, yrow, core, sib).wait_send()

time: 166 us -> 148 us (0.89); the launches traced: 163 us -> 147 us
  Pallas kernels: 160 us -> 145 us
    pallas_call x1, Pallas kernels: 160 us -> 145 us  [per_device(): pl.pallas_call(kernel, out_shape=jax.ShapeDtypeStruct((1, ROWS, COLS, CH)...]
where the time goes in v2:
time: 148 us; the launch traced here: 147 us
  Pallas kernels  145 us (98%)
  local copies, waits for them, and re-layouts  2.94 us (2%)
    pallas_call x1, Pallas kernels, per_device(): pl.pallas_call(kernel, out_shape=jax.ShapeDtypeStruct((1, ROWS, COLS, CH)...  145 us

profile of v2, /device:TPU:3, one launch (start us, length us, event | category | flops | bytes accessed | tf_op | source)
XLA Modules:
  0.0 147.5 jit_solution(1018759174049898031)
XLA Ops:
  0.0 144.5 %band_layer.1 = bf16[1,12,640,128]{3,2,1,0:T(8,128)(2,1)} custom-call(bf16[1,12,640,128]{3,2,1,0:T(8,128)(2,1)} %cells.1, f32[9,128]{1,0:T(8,128)} %conv_w.1, bf16[3,1024,128]{2,1,0:T(8,128)(2,1)} %wqkv.1, bf16[1024,128]{1,0:T(8,128)(2,1)} %wout.1, s32[6,20]{1,0:T(8,128)} %bmask.1), custom_call_target="tpu_custom_call" | custom-call | tf_op jit(solution)/shard_map/band_layer/pallas_call | solution.py:419
  144.6 2.9 %copy.7 = bf16[1,12,640,128]{3,2,1,0:T(8,128)(2,1)} copy(bf16[1,12,640,128]{3,2,1,0:T(8,128)(2,1)} %band_layer.1) | data formatting | bytes 3932160

commit v3 on v2

--- a/solution.py
+++ b/solution.py
@@ -23,7 +23,7 @@
 KROWS = ROWS + 6
 SLAB = 128
 AHEAD = 2
-EARLY = 3
+EARLY = 4
 NEG = -1e30
 EXP_SCALE = math.log2(math.e) / 8.0
 
@@ -32,7 +32,7 @@
     cells, conv_w, wqkv, wout, bmask, out,
     win, w4, cw, mixed, qbuf, kbuf, vbuf, att, ob,
     loc_sem, w_s, w_r, o_s, o_r, c_s, c_r, m_s, m_r, u_s, u_r, d_s, d_r,
-    y_s, y_r, r_s, r_r, rl_s,
+    y_s, y_r, r_s, r_r,
 ):
     t = lax.axis_index("tile")
     h = lax.axis_index("head")
@@ -43,17 +43,24 @@
     y_dn = (t + 12) % NT
     sib = t + 1 - 2 * core
     flip = 2 - 4 * low
-    not_top = t > 0
-    not_bot = t < NT - 1
+    tc = t + flip
+    not_top = tc > 0
+    not_bot = tc < NT - 1
+
+    def place_of(b):
+        return b + 2 - 4 * ((b // 2) % 2)
+
+    above = place_of((tc + NT - 1) % NT)
+    below = place_of((tc + 1) % NT)
 
     def slab_row(yy, cc):
         return pl.multiple_of(SLAB * (2 * yy + cc), SLAB)
 
-    @pl.when(t == 0)
+    @pl.when(tc == 0)
     def _():
         win[:, 0:4] = jnp.zeros((NH, 4, BC, CH), jnp.bfloat16)
 
-    @pl.when(t == NT - 1)
+    @pl.when(tc == NT - 1)
     def _():
         win[:, 16:20] = jnp.zeros((NH, 4, BC, CH), jnp.bfloat16)
 
@@ -70,20 +77,19 @@
         pl.semaphore_signal(bar, inc=1, device_id=(t, (h + k) % NH), device_id_type=MESH)
     for other in (y_up, y_dn):
         pl.semaphore_signal(bar, inc=1, device_id=(other, h), device_id_type=MESH)
-    for z in range(4):
-        far = 4 * (1 - h // 4) + z
-        pl.semaphore_signal(bar, inc=1, device_id=(t + flip, far), device_id_type=MESH)
+    for k in range(NH):
+        pl.semaphore_signal(bar, inc=1, device_id=(tc, (h + k) % NH), device_id_type=MESH)
 
     @pl.when(not_top)
     def _():
-        pl.semaphore_signal(bar, inc=1, device_id=(t - 1, h), device_id_type=MESH)
+        pl.semaphore_signal(bar, inc=1, device_id=(above, h), device_id_type=MESH)
 
     @pl.when(not_bot)
     def _():
-        pl.semaphore_signal(bar, inc=1, device_id=(t + 1, h), device_id_type=MESH)
+        pl.semaphore_signal(bar, inc=1, device_id=(below, h), device_id_type=MESH)
 
     bands_near = jnp.where(not_top, 1, 0) + jnp.where(not_bot, 1, 0)
-    pl.semaphore_wait(bar, NH - 1 + 2 + 4 + bands_near)
+    pl.semaphore_wait(bar, NH - 1 + 2 + NH + bands_near)
 
     def win_start(hd):
         return pl.multiple_of(jnp.clip(CW * hd - 8, 0, COLS - WC), 8)
@@ -121,7 +127,7 @@
             src_ref=cells.at[0, :, pl.ds(win_start(ht), WC), :],
             dst_ref=win.at[hs, 4:16, pl.ds(win_at(ht), WC), :],
             send_sem=m_s.at[k], recv_sem=m_r.at[k],
-            device_id=(t, ht), device_id_type=MESH)
+            device_id=(tc, ht), device_id_type=MESH)
 
     own_win = pl.ds(win_at(h), WC)
 
@@ -129,13 +135,13 @@
         return pltpu.make_async_remote_copy(
             src_ref=win.at[hs, 4:8, own_win, :], dst_ref=win.at[hs, 16:20, own_win, :],
             send_sem=u_s.at[k], recv_sem=u_r.at[k],
-            device_id=(t - 1, h), device_id_type=MESH)
+            device_id=(above, h), device_id_type=MESH)
 
     def d_copy(k, hs):
         return pltpu.make_async_remote_copy(
             src_ref=win.at[hs, 12:16, own_win, :], dst_ref=win.at[hs, 0:4, own_win, :],
             send_sem=d_s.at[k], recv_sem=d_r.at[k],
-            device_id=(t + 1, h), device_id_type=MESH)
+            device_id=(below, h), device_id_type=MESH)
 
     def pass_on(k):
         hs = (h + NH - k) % NH
@@ -156,9 +162,6 @@
             wout.at[pl.ds(own_rows, SLAB), :],
             w4.at[3, pl.ds(own_rows, SLAB), pl.ds(pl.multiple_of(CH * h, CH), CH)], loc_sem.at[1]),
         pltpu.make_async_copy(conv_w, cw.at[h], loc_sem.at[2]),
-        pltpu.make_async_copy(
-            cells.at[0, :, pl.ds(win_start(h), WC), :],
-            win.at[h, 4:16, pl.ds(win_at(h), WC), :], loc_sem.at[3]),
     ]
     for k in range(1, NH):
         ht = (h + k) % NH
@@ -168,10 +171,8 @@
         cp.start()
     for k in range(1, NH):
         c_copy(k, h, (h + k) % NH).start()
-    for k in range(1, NH):
+    for k in range(NH):
         m_copy(k, h, (h + k) % NH).start()
-    local[3].wait()
-    pass_on(0)
 
     def y_copy(idx, yy, cc, to, first=0, size=SLAB):
         rows = pl.ds(pl.multiple_of(slab_row(yy, cc) + first, size), size)
@@ -197,7 +198,7 @@
     y_copy(2, yrow, core, sib).start()
 
     local[2].wait()
-    for k in range(1, AHEAD):
+    for k in range(AHEAD):
         m_copy(k, (h + NH - k) % NH, h).wait_recv()
         pass_on(k)
 
@@ -309,19 +310,13 @@
             src_ref=ob.at[ht, pl.ds(2 * i, 2)],
             dst_ref=out.at[0, pl.ds(2 * i, 2), pl.ds(pl.multiple_of(CW * hs, 16), CW), :],
             send_sem=r_s.at[i, k], recv_sem=r_r.at[i, k],
-            device_id=(t, ht), device_id_type=MESH)
-
-    def r_local(i):
-        return pltpu.make_async_copy(
-            ob.at[h, pl.ds(2 * i, 2)],
-            out.at[0, pl.ds(2 * i, 2), pl.ds(pl.multiple_of(CW * h, 16), CW), :],
-            rl_s.at[i])
+            device_id=(tc, ht), device_id_type=MESH)
 
     def row_pair(i, carry):
         r0 = 2 * i
 
         def col_tile(j, c2):
-            row0 = ROWS * t - 3 + r0
+            row0 = ROWS * tc - 3 + r0
             col0 = CW * h - 8 + 16 * j
             rt = (row0 + 32) // 32 - 1
             ct = (col0 + 32) // 32 - 1
@@ -370,16 +365,14 @@
                 slab = win[dst, pl.ds(4 + r0, 2), 16:96, :].astype(jnp.float32)
                 res = slab + y[:, CH * m:CH * m + CH].reshape(2, CW, CH)
                 ob[dst, pl.ds(r0, 2)] = res.astype(jnp.bfloat16)
-        r_local(i).start()
-        for k in range(1, NH):
+        for k in range(NH):
             r_copy(i, k, h, (h + k) % NH).start()
         return carry
 
     lax.fori_loop(0, ROWS // 2, row_pair, 0)
 
     def drain(i, carry):
-        r_local(i).wait()
-        for k in range(1, NH):
+        for k in range(NH):
             r_copy(i, k, h, (h + k) % NH).wait_send()
             r_copy(i, k, (h + NH - k) % NH, h).wait_recv()
         return carry
@@ -389,9 +382,9 @@
         w_copy(k, h, ht).wait_send()
         o_copy(k, h, ht).wait_send()
         c_copy(k, h, ht).wait_send()
-        m_copy(k, h, ht).wait_send()
     for k in range(NH):
         hs = (h + NH - k) % NH
+        m_copy(k, h, (h + k) % NH).wait_send()
 
         @pl.when(not_top)
         def _():
@@ -431,11 +424,11 @@
             pltpu.VMEM((KROWS, WC, D), bf),
             pltpu.VMEM((2, CW, D), bf),
             pltpu.VMEM((NH, ROWS, CW, CH), bf),
-            sem((4,)),
+            sem((3,)),
             sem((NH,)), sem((NH,)), sem((NH,)), sem((NH,)), sem((NH,)), sem((NH,)),
             sem((NH,)), sem((NH,)), sem((NH,)), sem((NH,)), sem((NH,)), sem((NH,)),
             sem((8,)), sem((8,)),
-            sem((pairs, NH)), sem((pairs, NH)), sem((pairs,)),
+            sem((pairs, NH)), sem((pairs, NH)),
         ],
         compiler_params=pltpu.CompilerParams(
             collective_id=0, has_side_effects=True, vmem_limit_bytes=56 * 1024 * 1024),

time: 148 us -> 145 us (0.980)
  Pallas kernels: 145 us -> 142 us
    pallas_call x1, Pallas kernels: 145 us -> 142 us  [per_device(): pl.pallas_call(kernel, out_shape=jax.ShapeDtypeStruct((1, ROWS, COLS, CH)...]
where the time goes in v3:
time: 145 us
  Pallas kernels  142 us (98%)
  local copies, waits for them, and re-layouts  2.94 us (2%)
    pallas_call x1, Pallas kernels, per_device(): pl.pallas_call(kernel, out_shape=jax.ShapeDtypeStruct((1, ROWS, COLS, CH)...  142 us
    unnamed x1, local copies, waits for them, and re-layouts  2.94 us

profile of v3, /device:TPU:3, one launch (start us, length us, event | category | flops | bytes accessed | tf_op | source)
XLA Modules:
  0.0 145.1 jit_solution(4078063447251223301)
XLA Ops:
  0.0 142.2 %band_layer.1 = bf16[1,12,640,128]{3,2,1,0:T(8,128)(2,1)} custom-call(bf16[1,12,640,128]{3,2,1,0:T(8,128)(2,1)} %cells.1, f32[9,128]{1,0:T(8,128)} %conv_w.1, bf16[3,1024,128]{2,1,0:T(8,128)(2,1)} %wqkv.1, bf16[1024,128]{1,0:T(8,128)(2,1)} %wout.1, s32[6,20]{1,0:T(8,128)} %bmask.1), custom_call_target="tpu_custom_call" | custom-call | tf_op jit(solution)/shard_map/band_layer/pallas_call | solution.py:412
  142.2 2.9 %copy.7 = bf16[1,12,640,128]{3,2,1,0:T(8,128)(2,1)} copy(bf16[1,12,640,128]{3,2,1,0:T(8,128)(2,1)} %band_layer.1) | data formatting | bytes 3932160

commit v4 on v3

--- a/solution.py
+++ b/solution.py
@@ -22,8 +22,8 @@
 WROWS = ROWS + 8
 KROWS = ROWS + 6
 SLAB = 128
-AHEAD = 2
-EARLY = 4
+AHEAD = 4
+EARLY = 1
 NEG = -1e30
 EXP_SCALE = math.log2(math.e) / 8.0
 

time: 145 us -> 145 us (level)
  no operation moved by 1% of the time
where the time goes in v4:
time: 145 us
  Pallas kernels  142 us (98%)
  local copies, waits for them, and re-layouts  2.94 us (2%)
    pallas_call x1, Pallas kernels, per_device(): pl.pallas_call(kernel, out_shape=jax.ShapeDtypeStruct((1, ROWS, COLS, CH)...  142 us
    unnamed x1, local copies, waits for them, and re-layouts  2.94 us

profile of v4, /device:TPU:3, one launch (start us, length us, event | category | flops | bytes accessed | tf_op | source)
XLA Modules:
  0.0 144.9 jit_solution(1031454037836870238)
XLA Ops:
  0.0 142.0 %band_layer.1 = bf16[1,12,640,128]{3,2,1,0:T(8,128)(2,1)} custom-call(bf16[1,12,640,128]{3,2,1,0:T(8,128)(2,1)} %cells.1, f32[9,128]{1,0:T(8,128)} %conv_w.1, bf16[3,1024,128]{2,1,0:T(8,128)(2,1)} %wqkv.1, bf16[1024,128]{1,0:T(8,128)(2,1)} %wout.1, s32[6,20]{1,0:T(8,128)} %bmask.1), custom_call_target="tpu_custom_call" | custom-call | tf_op jit(solution)/shard_map/band_layer/pallas_call | solution.py:412
  142.0 2.9 %copy.7 = bf16[1,12,640,128]{3,2,1,0:T(8,128)(2,1)} copy(bf16[1,12,640,128]{3,2,1,0:T(8,128)(2,1)} %band_layer.1) | data formatting | bytes 3932160
